TPU v7x, 256 devices: a whole 4x4x8 slice. The times are simulated.
256 devices in a mesh: grp: 4 (over y), tok: 64 (over z, x, core).
Axes of the slice: x: 4, y: 4, z: 8, core: 2. Of those that a mesh axis runs over, the one named last changes fastest.
Arguments:
- hidden: bfloat16 [512, 64, 1024], P('tok', 'grp'), may hold values from -6 to 6
- draft_qkv: bfloat16 [3, 512, 64, 1024], P(None, 'tok', None, 'grp'), may hold values from -4 to 4
- self_cache: bfloat16 [512, 2, 512, 1024], P('tok', None, None, 'grp'), may hold values from -4 to 4
- cross_cache: bfloat16 [512, 2, 512, 1024], P('tok', None, None, 'grp'), may hold values from -4 to 4
- parents: int32 [512, 64], P('tok'), may hold values from -1 to 62, as said below
- counts: int32 [512], P('tok'), may hold values from 32 to 64, as said below
- self_len: int32 [512], P('tok'), may hold values from 2 to 512, as said below
- enc_len: int32 [512], P('tok'), may hold values from 2 to 512, as said below
- buckets: int32 [512, 64, 64], P('tok'), may hold values from 0 to 31
- bias_table: float32 [32, 16], P(None, 'grp'), may hold values from -4 to 4
- gain_cross: float32 [1024], replicated, may hold values from 0.25 to 1.75
- gain_ffn: float32 [1024], replicated, may hold values from 0.25 to 1.75
- gain_next: float32 [1024], replicated, may hold values from 0.25 to 1.75
- w_out_self: bfloat16 [1024, 1024], P('grp', 'tok'), may hold values from -0.1875 to 0.1875
- w_query_cross: bfloat16 [1024, 1024], P('tok', 'grp'), may hold values from -1 to 1
- w_out_cross: bfloat16 [1024, 1024], P('grp', 'tok'), may hold values from -0.1875 to 0.1875
- w_gate: bfloat16 [1024, 2816], P('tok', 'grp'), may hold values from -0.1875 to 0.1875
- w_up: bfloat16 [1024, 2816], P('tok', 'grp'), may hold values from -0.1875 to 0.1875
- w_down: bfloat16 [2816, 1024], P('grp', 'tok'), may hold values from -0.109375 to 0.109375
- w_qkv: bfloat16 [1024, 3, 1024], P('tok', None, 'grp'), may hold values from -0.1875 to 0.1875
Outputs:
- out_hidden: bfloat16 [512, 64, 1024], P('tok', 'grp')
- next_qkv: bfloat16 [3, 512, 64, 1024], P(None, 'tok', None, 'grp')
Inputs may be any that keep to these rules, and one draw needn't show every extreme that they name: `parents`: slot 0 of every tree has parent -1; every other slot's parent is an earlier slot. `counts`: some request fills all 64 draft slots. `self_len`: some request fills its whole cache. `enc_len`: some request has all 512 encoder positions.
All inputs are finite; a program needn't handle non-finite values.
Results may differ from a plain program's by a relative error of at most 0.025.
Values may be sent and summed in bfloat16 or wider, within the bound.
A program may use at most 64 MiB of HBM per device.

v0:
```python
import jax
import jax.numpy as jnp
from jax import lax
from jax.sharding import PartitionSpec as P

DH = 64


def ancestor_table(parent_ids):
    count_slots = parent_ids.shape[0]
    slot_ids = jnp.arange(count_slots, dtype=jnp.int32)
    ancestors = jnp.eye(count_slots, dtype=jnp.float32) + (
        parent_ids[:, None] == slot_ids[None, :]
    ).astype(jnp.float32)
    for repeat in range(max(1, count_slots.bit_length())):
        ancestors = jnp.minimum(jnp.dot(ancestors, ancestors, precision=lax.Precision.HIGHEST), 1.0)
    return ancestors


def rms_scale(stream, gain_vec):
    mean_square = jnp.mean(stream * stream, axis=-1, keepdims=True)
    return (stream * lax.rsqrt(mean_square + 1e-06) * gain_vec).astype(jnp.bfloat16)


def draft_attention(projected, cached, parent_ids, draft_count, length, bucket_ids, bias_table):
    requests, draft_slots, head_width = (projected.shape[1], projected.shape[2], projected.shape[3])
    local_heads = bias_table.shape[1]
    head_size = head_width // local_heads
    queries = projected[0].reshape(requests, draft_slots, local_heads, head_size)
    draft_keys = projected[1].reshape(requests, draft_slots, local_heads, head_size)
    draft_values = projected[2].reshape(requests, draft_slots, local_heads, head_size)
    cache_keys = cached[:, 0].reshape(requests, -1, local_heads, head_size)
    cache_values = cached[:, 1].reshape(requests, -1, local_heads, head_size)
    cache_scores = jnp.einsum(
        "rihd,rphd->rhip", queries, cache_keys, preferred_element_type=jnp.float32
    )
    cache_scores = cache_scores + bias_table[-1][None, :, None, None]
    cache_live = jnp.arange(cache_keys.shape[1], dtype=jnp.int32)[None, :] < length[:, None]
    cache_scores = jnp.where(cache_live[:, None, None, :], cache_scores, -1e30)
    onehot = (bucket_ids[..., None] == jnp.arange(bias_table.shape[0], dtype=jnp.int32)).astype(
        jnp.float32
    )
    draft_bias = jnp.einsum("rijb,bh->rhij", onehot, bias_table, precision=lax.Precision.HIGHEST)
    draft_scores = (
        jnp.einsum("rihd,rjhd->rhij", queries, draft_keys, preferred_element_type=jnp.float32)
        + draft_bias
    )
    ancestors = jax.vmap(ancestor_table)(parent_ids)
    draft_live = (ancestors > 0.5) & (
        jnp.arange(draft_slots, dtype=jnp.int32)[None, None, :] < draft_count[:, None, None]
    )
    draft_scores = jnp.where(draft_live[:, None], draft_scores, -1e30)
    highest = jnp.maximum(cache_scores.max(-1, keepdims=True), draft_scores.max(-1, keepdims=True))
    exp_cache = jnp.exp(cache_scores - highest)
    exp_draft = jnp.exp(draft_scores - highest)
    denominator = exp_cache.sum(-1, keepdims=True) + exp_draft.sum(-1, keepdims=True)
    weights_cache = (exp_cache / denominator).astype(jnp.bfloat16)
    weights_draft = (exp_draft / denominator).astype(jnp.bfloat16)
    attended = jnp.einsum(
        "rhip,rphd->rihd", weights_cache, cache_values, preferred_element_type=jnp.float32
    )
    attended = attended + jnp.einsum(
        "rhij,rjhd->rihd", weights_draft, draft_values, preferred_element_type=jnp.float32
    )
    return attended.astype(jnp.bfloat16).reshape(requests * draft_slots, head_width)


def cross_attention(query_rows, cached, length):
    requests, draft_slots, head_width = query_rows.shape
    local_heads = head_width // DH
    queries = query_rows.reshape(requests, draft_slots, local_heads, DH)
    enc_keys = cached[:, 0].reshape(requests, -1, local_heads, DH)
    enc_values = cached[:, 1].reshape(requests, -1, local_heads, DH)
    scores = jnp.einsum("rihd,rphd->rhip", queries, enc_keys, preferred_element_type=jnp.float32)
    live = jnp.arange(enc_keys.shape[1], dtype=jnp.int32)[None, :] < length[:, None]
    scores = jnp.where(live[:, None, None, :], scores, -1e30)
    highest = scores.max(-1, keepdims=True)
    exp_scores = jnp.exp(scores - highest)
    weights = (exp_scores / exp_scores.sum(-1, keepdims=True)).astype(jnp.bfloat16)
    attended = jnp.einsum(
        "rhip,rphd->rihd", weights, enc_values, preferred_element_type=jnp.float32
    )
    return attended.astype(jnp.bfloat16).reshape(requests * draft_slots, head_width)


def layer_sum(summand, base_full):
    return lax.psum(summand.astype(jnp.bfloat16), "grp").astype(jnp.float32) + base_full


def normed_rows(stream, gain_vec):
    scaled = rms_scale(stream, gain_vec)
    return scaled.reshape(-1, scaled.shape[-1])


def shards(
    hidden,
    draft_qkv,
    self_cache,
    cross_cache,
    parents,
    counts,
    self_len,
    enc_len,
    buckets,
    bias_table,
    gain_cross,
    gain_ffn,
    gain_next,
    w_out_self,
    w_query_cross,
    w_out_cross,
    w_gate,
    w_up,
    w_down,
    w_qkv,
):
    requests, share_rows, model_width = hidden.shape
    draft_slots = draft_qkv.shape[2]
    head_width = draft_qkv.shape[3]
    fetched = (
        lax.all_gather(w_out_self, "tok", axis=1, tiled=True),
        lax.all_gather(w_query_cross, "tok", axis=0, tiled=True),
        lax.all_gather(w_out_cross, "tok", axis=1, tiled=True),
        lax.all_gather(w_gate, "tok", axis=0, tiled=True),
        lax.all_gather(w_up, "tok", axis=0, tiled=True),
        lax.all_gather(w_down, "tok", axis=1, tiled=True),
        lax.all_gather(w_qkv, "tok", axis=0, tiled=True),
    )
    self_context = draft_attention(
        draft_qkv, self_cache, parents, counts, self_len, buckets, bias_table
    )
    partial_value = jnp.dot(self_context, fetched[0], preferred_element_type=jnp.float32)
    partial_value = partial_value.reshape(requests, draft_slots, model_width)
    own_rows = hidden.astype(jnp.float32)
    offset = lax.axis_index("grp") * share_rows
    placed = lax.dynamic_update_slice(
        jnp.zeros((requests, draft_slots, model_width), jnp.float32), own_rows, (0, offset, 0)
    )
    stream_one = layer_sum(partial_value + placed, 0.0)
    normed_one = normed_rows(stream_one, gain_cross)
    cross_query = jnp.dot(normed_one, fetched[1], preferred_element_type=jnp.float32)
    cross_query = cross_query.astype(jnp.bfloat16).reshape(requests, draft_slots, head_width)
    cross_context = cross_attention(cross_query, cross_cache, enc_len)
    partial_value = jnp.dot(cross_context, fetched[2], preferred_element_type=jnp.float32)
    stream_two = layer_sum(partial_value.reshape(requests, draft_slots, model_width), stream_one)
    normed_two = normed_rows(stream_two, gain_ffn)
    gate_part = jnp.dot(normed_two, fetched[3], preferred_element_type=jnp.float32)
    up_part = jnp.dot(normed_two, fetched[4], preferred_element_type=jnp.float32)
    gated = (jax.nn.gelu(gate_part, approximate=True) * up_part).astype(jnp.bfloat16)
    partial_value = jnp.dot(gated, fetched[5], preferred_element_type=jnp.float32)
    stream_three = layer_sum(partial_value.reshape(requests, draft_slots, model_width), stream_two)
    normed_three = normed_rows(stream_three, gain_next)
    projected = jnp.dot(
        normed_three,
        fetched[6].reshape(fetched[6].shape[0], -1),
        preferred_element_type=jnp.float32,
    )
    projected = projected.astype(jnp.bfloat16).reshape(requests, draft_slots, 3, head_width)
    next_qkv = jnp.transpose(projected, (2, 0, 1, 3))
    out_hidden = lax.dynamic_slice_in_dim(stream_three, offset, share_rows, 1).astype(jnp.bfloat16)
    return (out_hidden, next_qkv)


def solution(mesh):
    in_specs = (
        P("tok", "grp", None),
        P(None, "tok", None, "grp"),
        P("tok", None, None, "grp"),
        P("tok", None, None, "grp"),
        P("tok", None),
        P("tok"),
        P("tok"),
        P("tok"),
        P("tok", None, None),
        P(None, "grp"),
        P(),
        P(),
        P(),
        P("grp", "tok"),
        P("tok", "grp"),
        P("grp", "tok"),
        P("tok", "grp"),
        P("tok", "grp"),
        P("grp", "tok"),
        P("tok", None, "grp"),
    )
    out_specs = (P("tok", "grp", None), P(None, "tok", None, "grp"))
    return jax.shard_map(shards, mesh=mesh, in_specs=in_specs, out_specs=out_specs, check_vma=False)
```

profile of v0, /device:TPU:1, one launch (start us, length us, event | category | flops | bytes accessed | tf_op | source)
XLA Modules:
  0.0 532.7 jit_solution(6397232074818495033)
XLA Ops:
  8.1 3.9 fusion.56
  12.0 2.4 copy.53
  14.6 2.9 copy.47
  17.5 1.9 fusion.57
  19.4 0.2 reshape_squeeze.21
  19.7 3.6 fusion.1
  23.3 2.6 copy.52
  25.8 1.2 reshape_squeeze.23
  27.1 0.5 convolution_minimum_fusion.6
  27.6 0.4 convolution_minimum_fusion.5
  28.0 0.4 convolution_minimum_fusion.4
  28.4 0.4 convolution_minimum_fusion.3
  28.8 0.4 convolution_minimum_fusion.2
  29.2 0.4 convolution_minimum_fusion.1
  29.7 0.4 fusion.29
  30.3 0.8 fusion.3
  31.0 0.4 copy-done.3
  31.5 0.4 fusion.58
  32.0 1.5 fusion.7
  33.7 1.0 reshape_squeeze.25
  34.7 3.0 fusion.14
  37.8 0.4 fusion.27
  38.2 0.4 copy.56
  38.6 0.3 dot_general.79
  39.0 54.8 %all_gather.21 = bf16[256,1024]{0,1:T(8,128)(2,1)S(1)} all-gather(bf16[256,16]{0,1:T(8,128)(2,1)S(1)} %copy-done.9), channel_id=1, replica_groups=mesh['grp'=4,'tok'=64] {'tok'}, dimensions={1}, use_global_device_ids=true | all-gather | bytes 532480 | tf_op jit(solution)/shard_map/all_gather | solution.py:121
  93.8 0.5 fusion.32
  94.4 1.1 convert_element_type.84
  95.6 3.9 fusion.55
  99.5 2.4 copy.59
  101.9 2.9 copy.57
  104.8 49.2 %all_gather.22 = bf16[1024,256]{1,0:T(8,128)(2,1)S(1)} all-gather(bf16[16,256]{1,0:T(8,128)(2,1)S(1)} %copy-done.10), channel_id=1, replica_groups=mesh['grp'=4,'tok'=64] {'tok'}, dimensions={0}, use_global_device_ids=true | all-gather | bytes 532480 | tf_op jit(solution)/shard_map/all_gather | solution.py:122
  154.0 48.2 %all_gather.23 = bf16[256,1024]{0,1:T(8,128)(2,1)S(1)} all-gather(bf16[256,16]{0,1:T(8,128)(2,1)S(1)} %copy-done.11), channel_id=1, replica_groups=mesh['grp'=4,'tok'=64] {'tok'}, dimensions={1}, use_global_device_ids=true | all-gather | bytes 532480 | tf_op jit(solution)/shard_map/all_gather | solution.py:123
  202.2 1.5 fusion.8
  203.8 1.5 fusion.10
  205.3 0.4 convolution_convert_fusion.3
  205.7 0.2 reshape_reshape.3
  206.0 0.7 fusion.34
  206.7 2.0 fusion.59
  208.7 0.8 fusion.26
  209.4 0.4 copy.60
  209.9 0.3 dot_general.84
  210.2 1.5 convolution_convert_fusion.1
  211.8 0.5 all-gather.5.cloned.1.call-update
  212.4 0.5 all-gather.9.cloned.1.call-update
  213.0 0.5 all-gather.7.cloned.1.call-update
  213.6 0.7 all-gather.11.cloned.1.call-update
  214.3 0.3 all-reduce.8.cloned.1.call-start
  214.6 44.3 %all-reduce.6.cloned.1.call-done = bf16[8,64,1024]{2,1,0:T(8,128)(2,1)} async-done(((bf16[8,64,1024]{2,1,0:T(8,128)(2,1)}), bf16[8,64,1024]{2,1,0:T(8,128)(2,1)}) %all-reduce.6.cloned.1.call-update) | async-done | bytes 1048592 | tf_op jit(solution)/shard_map/psum | solution.py:87
  258.9 1.7 multiply_reduce_fusion.1
  260.6 0.4 multiply_convert_fusion.1
  261.0 28.7 %all-gather.5.cloned.1.call-done = bf16[1024,704]{1,0:T(8,128)(2,1)} async-done(((bf16[16,704]{1,0:T(8,128)(2,1)}), bf16[1024,704]{1,0:T(8,128)(2,1)}) %all-gather.5.cloned.1.call-update) | async-done | bytes 1441808 | tf_op jit(solution)/shard_map/all_gather | solution.py:124
  289.7 3.5 fusion.60
  293.2 73.9 %all-gather.9.cloned.1.call-done = bf16[704,1024]{0,1:T(8,128)(2,1)} async-done(((bf16[704,16]{0,1:T(8,128)(2,1)}), bf16[704,1024]{0,1:T(8,128)(2,1)}) %all-gather.9.cloned.1.call-update) | async-done | bytes 1441808 | tf_op jit(solution)/shard_map/all_gather | solution.py:126
  367.1 77.4 %all-gather.7.cloned.1.call-done = bf16[1024,704]{1,0:T(8,128)(2,1)} async-done(((bf16[16,704]{1,0:T(8,128)(2,1)}), bf16[1024,704]{1,0:T(8,128)(2,1)}) %all-gather.7.cloned.1.call-update) | async-done | bytes 1441808 | tf_op jit(solution)/shard_map/all_gather | solution.py:125
  444.5 5.5 %convolution_convert_fusion = bf16[512,1024]{1,0:T(8,128)(2,1)} fusion(bf16[704,1024]{0,1:T(8,128)(2,1)} %all-gather.9.cloned.1.call-done, bf16[512,1024]{1,0:T(8,128)(2,1)S(1)} %bitcast.67, bf16[1024,704]{1,0:T(8,128)(2,1)} %all-gather.7.cloned.1.call-done, f32[512,704]{0,1:T(8,128)} %fusion.60), kind=kOutput, calls=%fused_computation.29 | convolution fusion | flops 1480523776 | bytes 6422528 | tf_op jit(solution)/shard_map/dot_general | solution.py:150
  450.0 67.0 %all-gather.11.cloned.1.call-done = bf16[1024,3,256]{2,0,1:T(8,128)(2,1)} async-done(((bf16[16,3,256]{2,0,1:T(8,128)(2,1)}), bf16[1024,3,256]{2,0,1:T(8,128)(2,1)}) %all-gather.11.cloned.1.call-update) | async-done | bytes 1572880 | tf_op jit(solution)/shard_map/all_gather | solution.py:127
  517.1 2.6 copy.61
  519.7 1.8 multiply_reduce_fusion
  521.4 0.7 dynamic-slice_convert_fusion
  522.2 0.2 multiply_convert_fusion
  522.4 0.5 copy-done.6
  522.9 1.0 convolution_convert_fusion.2
  524.0 0.4 reshape.141
  524.4 1.0 copy.62
  (64 shorter events, 1.3 us)
Async XLA Ops:
  8.0 194.2 %all-reduce.4.cloned.1.call-start = ((), (), s32[]{:S(2)}) async-start(), calls=%async_computation | async-start | bytes 2097152 | tf_op jit(solution)/shard_map/psum | solution.py:87
  12.0 2.4 copy-start.16
  12.0 2.6 copy-start.17
  17.5 2.2 copy-start.19
  19.7 7.4 %copy-start.12 = (s32[8,64]{1,0:T(8,128)S(1)}, s32[8,64]{1,0:T(8,128)}, u32[]{:S(2)}) copy-start(s32[8,64]{1,0:T(8,128)} %param.24) | copy-start | bytes 6148
  27.1 2.5 copy-start.20
  30.3 1.2 copy-start.3
  31.5 2.0 copy-start.1
  31.9 2.8 copy-start.4
  34.7 3.1 copy-start.7
  37.8 1.2 copy-start.9
  38.6 55.7 %copy-start.8 = (bf16[8,16,1024]{2,1,0:T(8,128)(2,1)S(1)}, bf16[8,16,1024]{2,1,0:T(8,128)(2,1)}, u32[]{:S(2)}) copy-start(bf16[8,16,1024]{2,1,0:T(8,128)(2,1)} %param.20) | copy-start | bytes 786436
  95.6 163.3 %all-reduce.6.cloned.1.call-start = ((), (), s32[]{:S(2)}) async-start(), calls=%async_computation.1 | async-start | bytes 2097152 | tf_op jit(solution)/shard_map/psum | solution.py:87
  101.9 2.9 copy-start.10
  101.9 52.1 %copy-start.11 = (bf16[256,16]{0,1:T(8,128)(2,1)S(1)}, bf16[256,16]{0,1:T(8,128)(2,1)}, u32[]{:S(2)}) copy-start(bf16[256,16]{0,1:T(8,128)(2,1)} %param.35) | copy-start | bytes 24580
  101.9 100.3 %copy-start.18 = (s32[8]{0:T(128)S(1)}, s32[8]{0:T(128)}, u32[]{:S(2)}) copy-start(s32[8]{0:T(128)} %param.27) | copy-start | bytes 100
  104.8 98.9 %copy-start.13 = (f32[1024]{0:T(1024)S(1)}, f32[1024]{0:T(1024)}, u32[]{:S(2)}) copy-start(f32[1024]{0:T(1024)} %param.30) | copy-start | bytes 12292
  206.7 2.0 copy-start.5
  209.9 49.0 %copy-start = (bf16[8,64,1024]{2,1,0:T(8,128)(2,1)S(1)}, bf16[8,64,1024]{2,1,0:T(8,128)(2,1)}, u32[]{:S(2)}) copy-start(bf16[8,64,1024]{2,1,0:T(8,128)(2,1)} %all-reduce.4.cloned.1.call-done) | copy-start | bytes 3145732
  210.2 50.4 %copy-start.14 = (f32[1024]{0:T(1024)S(1)}, f32[1024]{0:T(1024)}, u32[]{:S(2)}) copy-start(f32[1024]{0:T(1024)} %param.31) | copy-start | bytes 12292
  211.8 77.9 %all-gather.5.cloned.1.call-start = ((), (), s32[]{:S(2)}) async-start(), calls=%async_computation.2 | async-start | bytes 1597440 | tf_op jit(solution)/shard_map/all_gather | solution.py:124
  212.4 154.7 %all-gather.9.cloned.1.call-start = ((), (), s32[]{:S(2)}) async-start(), calls=%async_computation.4 | async-start | bytes 1597440 | tf_op jit(solution)/shard_map/all_gather | solution.py:126
  213.0 231.5 %all-gather.7.cloned.1.call-start = ((), (), s32[]{:S(2)}) async-start(), calls=%async_computation.3 | async-start | bytes 1597440 | tf_op jit(solution)/shard_map/all_gather | solution.py:125
  213.5 303.5 %all-gather.11.cloned.1.call-start = ((), (), s32[]{:S(2)}) async-start(), calls=%async_computation.6 | async-start | bytes 1597440 | tf_op jit(solution)/shard_map/all_gather | solution.py:127
  214.3 305.4 %all-reduce.8.cloned.1.call-start = ((), (), s32[]{:S(2)}) async-start(), calls=%async_computation.5 | async-start | bytes 2097152 | tf_op jit(solution)/shard_map/psum | solution.py:87
  258.9 1.7 copy-start.2
  519.6 2.5 copy-start.15
  521.4 1.5 copy-start.6
Sparse Core Ops, SparseCore 0:
  95.7 46.8 all-reduce.3
  211.9 46.8 all-reduce.5
  450.1 46.8 all-reduce.7
Sparse Core Ops, SparseCore 1:
  215.0 74.7 all-gather.4
  292.4 74.7 all-gather.8
  369.8 74.7 all-gather.6
  447.5 69.5 all-gather.10
where the time goes:
time: 533 us
  waiting for transfers between devices  294 us (55%)
  blocking collectives  152 us (29%)
  local copies, waits for them, and re-layouts  33.2 us (6%)
  matrix products  25 us (5%)
  between operations  15.9 us (3%)
  other arithmetic  12.3 us (2%)
    all_gather x1, waiting for transfers between devices, shards(): lax.all_gather(w_up, 'tok', axis=0, tiled=True)  77.4 us
    all_gather x1, waiting for transfers between devices, shards(): lax.all_gather(w_down, 'tok', axis=1, tiled=True)  73.9 us
    all_gather x1, waiting for transfers between devices, shards(): lax.all_gather(w_qkv, 'tok', axis=0, tiled=True)  67 us
    all_gather x1, blocking collectives, shards(): lax.all_gather(w_out_self, 'tok', axis=1, tiled=True)  54.8 us
    all_gather x1, blocking collectives, shards(): lax.all_gather(w_query_cross, 'tok', axis=0, tiled=True)  49.2 us
    all_gather x1, blocking collectives, shards(): lax.all_gather(w_out_cross, 'tok', axis=1, tiled=True)  48.2 us
    psum x3, waiting for transfers between devices, layer_sum(): lax.psum(summand.astype(jnp.bfloat16), 'grp').astype(jnp.float32)  44.3 us
    all_gather x1, waiting for transfers between devices, shards(): lax.all_gather(w_gate, 'tok', axis=0, tiled=True)  28.7 us
  transfers between devices with their start and end apart: 7, of which 5 were waited for; matrix products, arithmetic and copies ran while one was open for 4% of the time, Pallas kernels for 0%

commit v1 on v0

--- a/solution.py
+++ b/solution.py
@@ -120,7 +120,9 @@
     fetched = (
         lax.all_gather(w_out_self, "tok", axis=1, tiled=True),
         lax.all_gather(w_query_cross, "tok", axis=0, tiled=True),
-        lax.all_gather(w_out_cross, "tok", axis=1, tiled=True),
+        jnp.concatenate(
+            lax.all_to_all(jnp.stack([w_out_cross] * lax.axis_size("tok")), "tok", 0, 0), axis=1
+        ),
         lax.all_gather(w_gate, "tok", axis=0, tiled=True),
         lax.all_gather(w_up, "tok", axis=0, tiled=True),
         lax.all_gather(w_down, "tok", axis=1, tiled=True),

time: 533 us -> 496 us (0.931)
  blocking collectives: 152 us -> 106 us
  starting transfers between devices: 0.55 us -> 6.96 us
    all_gather x1 -> x0, blocking collectives: 48.2 us -> none  [shards(): lax.all_gather(w_out_cross, 'tok', axis=1, tiled=True)]
    all_to_all x0 -> x1, starting transfers between devices: none -> 6.46 us  [shards(): lax.all_to_all(jnp.stack([w_out_cross] * lax.axis_size('tok')), 'tok', 0, 0)]
  transfers between devices with their start and end apart: 7 -> 8, of which waited for: 5 -> 5; matrix products, arithmetic and copies ran while one was open for 4% -> 6% of each run, Pallas kernels for 0% -> 0%
where the time goes in v1:
time: 496 us; the launch traced here: 495 us
  waiting for transfers between devices  295 us (59%)
  blocking collectives  106 us (21%)
  local copies, waits for them, and re-layouts  34.2 us (7%)
  matrix products  24.9 us (5%)
  between operations  15.9 us (3%)
  other arithmetic  12.3 us (2%)
  starting transfers between devices  6.96 us (1%)
    all_gather x1, waiting for transfers between devices, shards(): lax.all_gather(w_up, 'tok', axis=0, tiled=True)  77.4 us
    all_gather x1, waiting for transfers between devices, shards(): lax.all_gather(w_down, 'tok', axis=1, tiled=True)  73.9 us
    all_gather x1, waiting for transfers between devices, shards(): lax.all_gather(w_qkv, 'tok', axis=0, tiled=True)  67.1 us
    all_gather x1, blocking collectives, shards(): lax.all_gather(w_out_self, 'tok', axis=1, tiled=True)  54.8 us
    all_gather x1, blocking collectives, shards(): lax.all_gather(w_query_cross, 'tok', axis=0, tiled=True)  51.2 us
    psum x3, waiting for transfers between devices, layer_sum(): lax.psum(summand.astype(jnp.bfloat16), 'grp').astype(jnp.float32)  45.1 us
    all_gather x1, waiting for transfers between devices, shards(): lax.all_gather(w_gate, 'tok', axis=0, tiled=True)  28.8 us
  transfers between devices with their start and end apart: 8, of which 5 were waited for; matrix products, arithmetic and copies ran while one was open for 6% of the time, Pallas kernels for 0%

profile of v1, /device:TPU:1, one launch (start us, length us, event | category | flops | bytes accessed | tf_op | source)
XLA Modules:
  0.0 494.9 jit_solution(7325701304435429074)
XLA Ops:
  8.1 3.9 fusion.55
  12.0 2.4 copy.55
  14.6 2.9 copy.49
  17.5 1.9 fusion.56
  19.7 3.6 fusion.1
  23.3 2.6 copy.54
  25.8 1.2 reshape_squeeze.23
  27.1 0.5 convolution_minimum_fusion.6
  27.6 0.4 convolution_minimum_fusion.5
  28.0 0.4 convolution_minimum_fusion.4
  28.4 0.4 convolution_minimum_fusion.3
  28.8 0.4 convolution_minimum_fusion.2
  29.2 0.4 convolution_minimum_fusion.1
  29.7 0.4 fusion.29
  30.3 0.8 fusion.3
  31.0 0.4 copy-done.3
  31.5 0.4 fusion.57
  31.9 1.5 fusion.7
  33.7 1.0 reshape_squeeze.25
  34.7 3.0 fusion.14
  37.8 0.4 fusion.27
  38.2 0.4 copy.58
  38.6 0.3 dot_general.79
  39.0 54.8 %all_gather.18 = bf16[256,1024]{0,1:T(8,128)(2,1)S(1)} all-gather(bf16[256,16]{0,1:T(8,128)(2,1)S(1)} %copy-done.9), channel_id=1, replica_groups=mesh['grp'=4,'tok'=64] {'tok'}, dimensions={1}, use_global_device_ids=true | all-gather | bytes 532480 | tf_op jit(solution)/shard_map/all_gather | solution.py:121
  93.8 0.5 fusion.31
  94.4 1.1 convert_element_type.84
  95.6 0.8 stack.2
  96.4 6.5 %all-to-all-start = ((bf16[64,256,16]{1,2,0:T(8,128)(2,1)}), bf16[64,256,16]{1,2,0:T(8,128)(2,1)S(1)}, u32[]{:S(2)}, u32[]{:S(2)}) async-start(bf16[64,256,16]{1,2,0:T(8,128)(2,1)} %stack.2), calls=%async_computation | async-start | bytes 1048576 | tf_op jit(solution)/shard_map/all_to_all | solution.py:124
  102.9 4.1 fusion.54
  107.0 2.4 copy.61
  109.4 2.9 copy.59
  112.3 51.2 %all_gather.19 = bf16[1024,256]{1,0:T(8,128)(2,1)S(1)} all-gather(bf16[16,256]{1,0:T(8,128)(2,1)S(1)} %copy-done.11), channel_id=1, replica_groups=mesh['grp'=4,'tok'=64] {'tok'}, dimensions={0}, use_global_device_ids=true | all-gather | bytes 532480 | tf_op jit(solution)/shard_map/all_gather | solution.py:122
  163.6 1.5 fusion.8
  165.1 1.5 fusion.10
  166.6 0.4 convolution_convert_fusion.3
  167.1 0.2 reshape_reshape.3
  167.3 0.7 fusion.33
  168.0 2.0 fusion.58
  170.0 0.8 fusion.26
  170.8 0.4 copy.62
  171.2 0.3 dot_general.84
  171.6 1.5 convolution_convert_fusion.1
  173.2 0.5 all-gather.5.cloned.1.call-update
  173.7 0.5 all-gather.9.cloned.1.call-update
  174.3 0.5 all-gather.7.cloned.1.call-update
  174.9 0.7 all-gather.11.cloned.1.call-update
  175.6 0.3 all-reduce.8.cloned.1.call-start
  175.9 45.1 %all-reduce.6.cloned.1.call-done = bf16[8,64,1024]{2,1,0:T(8,128)(2,1)} async-done(((bf16[8,64,1024]{2,1,0:T(8,128)(2,1)}), bf16[8,64,1024]{2,1,0:T(8,128)(2,1)}) %all-reduce.6.cloned.1.call-update) | async-done | bytes 1048592 | tf_op jit(solution)/shard_map/psum | solution.py:87
  221.0 1.7 multiply_reduce_fusion.1
  222.7 0.4 multiply_convert_fusion.1
  223.1 28.8 %all-gather.5.cloned.1.call-done = bf16[1024,704]{1,0:T(8,128)(2,1)} async-done(((bf16[16,704]{1,0:T(8,128)(2,1)}), bf16[1024,704]{1,0:T(8,128)(2,1)}) %all-gather.5.cloned.1.call-update) | async-done | bytes 1441808 | tf_op jit(solution)/shard_map/all_gather | solution.py:126
  251.9 3.5 fusion.59
  255.3 73.9 %all-gather.9.cloned.1.call-done = bf16[704,1024]{0,1:T(8,128)(2,1)} async-done(((bf16[704,16]{0,1:T(8,128)(2,1)}), bf16[704,1024]{0,1:T(8,128)(2,1)}) %all-gather.9.cloned.1.call-update) | async-done | bytes 1441808 | tf_op jit(solution)/shard_map/all_gather | solution.py:128
  329.3 77.4 %all-gather.7.cloned.1.call-done = bf16[1024,704]{1,0:T(8,128)(2,1)} async-done(((bf16[16,704]{1,0:T(8,128)(2,1)}), bf16[1024,704]{1,0:T(8,128)(2,1)}) %all-gather.7.cloned.1.call-update) | async-done | bytes 1441808 | tf_op jit(solution)/shard_map/all_gather | solution.py:127
  406.7 5.5 %convolution_convert_fusion = bf16[512,1024]{1,0:T(8,128)(2,1)} fusion(bf16[704,1024]{0,1:T(8,128)(2,1)} %all-gather.9.cloned.1.call-done, bf16[512,1024]{1,0:T(8,128)(2,1)S(1)} %bitcast.71, bf16[1024,704]{1,0:T(8,128)(2,1)} %all-gather.7.cloned.1.call-done, f32[512,704]{0,1:T(8,128)} %fusion.59), kind=kOutput, calls=%fused_computation.29 | convolution fusion | flops 1480523776 | bytes 6422528 | tf_op jit(solution)/shard_map/dot_general | solution.py:152
  412.2 67.1 %all-gather.11.cloned.1.call-done = bf16[1024,3,256]{2,0,1:T(8,128)(2,1)} async-done(((bf16[16,3,256]{2,0,1:T(8,128)(2,1)}), bf16[1024,3,256]{2,0,1:T(8,128)(2,1)}) %all-gather.11.cloned.1.call-update) | async-done | bytes 1572880 | tf_op jit(solution)/shard_map/all_gather | solution.py:129
  479.2 2.6 copy.64
  481.8 1.8 multiply_reduce_fusion
  483.6 0.7 dynamic-slice_convert_fusion
  484.3 0.2 multiply_convert_fusion
  484.6 0.5 copy-done.6
  485.1 1.0 convolution_convert_fusion.2
  486.1 0.4 reshape.151
  486.5 1.0 copy.65
  (66 shorter events, 1.6 us)
Async XLA Ops:
  8.0 155.6 %all-reduce.4.cloned.1.call-start = ((), (), s32[]{:S(2)}) async-start(), calls=%async_computation.1 | async-start | bytes 2097152 | tf_op jit(solution)/shard_map/psum | solution.py:87
  12.0 2.4 copy-start.16
  12.0 2.6 copy-start.17
  17.5 2.2 copy-start.19
  19.7 7.4 %copy-start.12 = (s32[8,64]{1,0:T(8,128)S(1)}, s32[8,64]{1,0:T(8,128)}, u32[]{:S(2)}) copy-start(s32[8,64]{1,0:T(8,128)} %param.24) | copy-start | bytes 6148
  27.1 2.5 copy-start.20
  30.2 1.2 copy-start.3
  31.5 2.0 copy-start.1
  31.9 2.8 copy-start.4
  34.7 3.1 copy-start.7
  37.8 1.2 copy-start.9
  38.6 55.7 %copy-start.8 = (bf16[8,16,1024]{2,1,0:T(8,128)(2,1)S(1)}, bf16[8,16,1024]{2,1,0:T(8,128)(2,1)}, u32[]{:S(2)}) copy-start(bf16[8,16,1024]{2,1,0:T(8,128)(2,1)} %param.20) | copy-start | bytes 786436
  94.4 1.2 copy-start.10
  96.4 75.1 %all-to-all-start = ((bf16[64,256,16]{1,2,0:T(8,128)(2,1)}), bf16[64,256,16]{1,2,0:T(8,128)(2,1)S(1)}, u32[]{:S(2)}, u32[]{:S(2)}) async-start(bf16[64,256,16]{1,2,0:T(8,128)(2,1)} %stack.2), calls=%async_computation | async-start | bytes 1048576 | tf_op jit(solution)/shard_map/all_to_all | solution.py:124
  102.9 118.1 %all-reduce.6.cloned.1.call-start = ((), (), s32[]{:S(2)}) async-start(), calls=%async_computation.2 | async-start | bytes 2097152 | tf_op jit(solution)/shard_map/psum | solution.py:87
  109.4 2.9 copy-start.11
  109.4 54.1 %copy-start.18 = (s32[8]{0:T(128)S(1)}, s32[8]{0:T(128)}, u32[]{:S(2)}) copy-start(s32[8]{0:T(128)} %param.27) | copy-start | bytes 100
  109.4 55.7 %copy-start.13 = (f32[1024]{0:T(1024)S(1)}, f32[1024]{0:T(1024)}, u32[]{:S(2)}) copy-start(f32[1024]{0:T(1024)} %param.30) | copy-start | bytes 12292
  168.0 2.0 copy-start.5
  171.2 49.8 %copy-start = (bf16[8,64,1024]{2,1,0:T(8,128)(2,1)S(1)}, bf16[8,64,1024]{2,1,0:T(8,128)(2,1)}, u32[]{:S(2)}) copy-start(bf16[8,64,1024]{2,1,0:T(8,128)(2,1)} %all-reduce.4.cloned.1.call-done) | copy-start | bytes 3145732
  171.6 51.2 %copy-start.14 = (f32[1024]{0:T(1024)S(1)}, f32[1024]{0:T(1024)}, u32[]{:S(2)}) copy-start(f32[1024]{0:T(1024)} %param.31) | copy-start | bytes 12292
  173.1 78.8 %all-gather.5.cloned.1.call-start = ((), (), s32[]{:S(2)}) async-start(), calls=%async_computation.3 | async-start | bytes 1597440 | tf_op jit(solution)/shard_map/all_gather | solution.py:126
  173.7 155.6 %all-gather.9.cloned.1.call-start = ((), (), s32[]{:S(2)}) async-start(), calls=%async_computation.5 | async-start | bytes 1597440 | tf_op jit(solution)/shard_map/all_gather | solution.py:128
  174.3 232.4 %all-gather.7.cloned.1.call-start = ((), (), s32[]{:S(2)}) async-start(), calls=%async_computation.4 | async-start | bytes 1597440 | tf_op jit(solution)/shard_map/all_gather | solution.py:127
  174.9 304.3 %all-gather.11.cloned.1.call-start = ((), (), s32[]{:S(2)}) async-start(), calls=%async_computation.7 | async-start | bytes 1597440 | tf_op jit(solution)/shard_map/all_gather | solution.py:129
  175.6 306.2 %all-reduce.8.cloned.1.call-start = ((), (), s32[]{:S(2)}) async-start(), calls=%async_computation.6 | async-start | bytes 2097152 | tf_op jit(solution)/shard_map/psum | solution.py:87
  221.0 1.7 copy-start.2
  481.8 2.5 copy-start.15
  483.6 1.5 copy-start.6
Sparse Core Ops, SparseCore 0:
  95.7 46.8 all-reduce.3
  173.2 47.6 all-reduce.5
  412.3 46.8 all-reduce.7
Sparse Core Ops, SparseCore 1:
  176.3 75.5 all-gather.4
  254.5 74.7 all-gather.8
  331.9 74.7 all-gather.6
  409.7 69.5 all-gather.10
